TPU v7x, 32 devices: a whole 2x2x4 slice. The times are simulated.
32 devices in a mesh: fsdp: 2 (over y), ctx: 4 (over x, core), tp: 4 (over z).
Axes of the slice: x: 2, y: 2, z: 4, core: 2. Of those that a mesh axis runs over, the one named last changes fastest.
Arguments:
- tokens: bfloat16 [8, 2048, 1024], P('fsdp', 'ctx'), may hold values from -6 to 6
- segments: int32 [8, 2048], P('fsdp'), may hold values from 0 to 10, as said below
- w_qkv: bfloat16 [3, 1024, 1024], P(None, 'fsdp', 'tp'), may hold values from -0.1875 to 0.1875
- b_qv: bfloat16 [2, 16, 64], P(None, 'tp', 'fsdp'), may hold values from -3 to 3
- w_o: bfloat16 [1024, 1024], P('tp', 'fsdp'), may hold values from -3 to 3
- b_o: bfloat16 [1024], P('fsdp'), may hold values from -3 to 3
- ln1_gain: bfloat16 [1024], P('fsdp'), may hold values from 0.5 to 1.5
- ln1_bias: bfloat16 [1024], P('fsdp'), may hold values from -2 to 2
- w_in: bfloat16 [1024, 4096], P('fsdp', 'tp'), may hold values from -0.1875 to 0.1875
- b_in: bfloat16 [64, 64], P('tp', 'fsdp'), may hold values from -3 to 3
- w_out: bfloat16 [4096, 1024], P('tp', 'fsdp'), may hold values from -0.09375 to 0.09375
- b_out: bfloat16 [1024], P('fsdp'), may hold values from -3 to 3
- ln2_gain: bfloat16 [1024], P('fsdp'), may hold values from 0.5 to 1.5
- ln2_bias: bfloat16 [1024], P('fsdp'), may hold values from -2 to 2
- cotangent: bfloat16 [8, 2048, 1024], P('fsdp', 'ctx'), may hold values from -6 to 6
Outputs:
- output: bfloat16 [8, 2048, 1024], P('fsdp', 'ctx')
- grad_tokens: bfloat16 [8, 2048, 1024], P('fsdp', 'ctx')
- grad_w_qkv: float32 [3, 1024, 1024], P(None, 'fsdp', 'tp')
- grad_b_qv: float32 [2, 16, 64], P(None, 'tp', 'fsdp')
- grad_w_o: float32 [1024, 1024], P('tp', 'fsdp')
- grad_b_o: float32 [1024], P('fsdp')
- grad_ln1_gain: float32 [1024], P('fsdp')
- grad_ln1_bias: float32 [1024], P('fsdp')
- grad_w_in: float32 [1024, 4096], P('fsdp', 'tp')
- grad_b_in: float32 [64, 64], P('tp', 'fsdp')
- grad_w_out: float32 [4096, 1024], P('tp', 'fsdp')
- grad_b_out: float32 [1024], P('fsdp')
- grad_ln2_gain: float32 [1024], P('fsdp')
- grad_ln2_bias: float32 [1024], P('fsdp')
Inputs may be any that keep to these rules, and one draw needn't show every extreme that they name: `segments`: in each sequence the ids start at 0 and rise by one at each document boundary; every document has 200 to 2000 tokens except a sequence's last, which ends with the sequence and may be shorter; one document of the batch has exactly 2000 tokens, and one sequence is made of documents of exactly 200 tokens except its last.
All inputs are finite; a program needn't handle non-finite values.
Results may differ from a plain program's by a relative error of at most 0.02.
Values may be sent and summed in bfloat16 or wider, within the bound.
No kernel may reach another device: no remote copies, remote signals or barrier semaphores. Data moves between devices by JAX's collectives and lax.ppermute only.
A program may use at most 192 MiB of HBM per device.

v0:
```python
import jax
import jax.numpy as jnp
from jax import lax
from jax.sharding import PartitionSpec as P

EPSILON = 1e-12
NEG_LARGE = -1e30
SCALE_QK = 0.125


def layer_norm(values, gain_vec, offset):
    center = values - jnp.mean(values, -1, keepdims=True)
    spread = jnp.mean(center * center, -1, keepdims=True)
    return center * lax.rsqrt(spread + EPSILON) * gain_vec + offset


def gelu_exact(values):
    return 0.5 * values * (1.0 + jax.scipy.special.erf(values * 0.7071067811865476))


def to_heads(blocks, head_size):
    seq_count, row_len, col_count = blocks.shape
    return blocks.reshape(seq_count, row_len, col_count // head_size, head_size).transpose(
        2, 0, 1, 3
    )


def from_heads(blocks):
    head_count, seq_count, row_len, head_size = blocks.shape
    return blocks.transpose(1, 2, 0, 3).reshape(seq_count, row_len, head_count * head_size)


def masked_scores(query_head, key_head, same_doc):
    scores = (
        jnp.einsum("sqd,skd->sqk", query_head, key_head, preferred_element_type=jnp.float32)
        * SCALE_QK
    )
    return jnp.where(same_doc, scores, NEG_LARGE)


def local(
    tokens,
    segments,
    w_qkv,
    b_qv,
    w_o,
    b_o,
    ln1_gain,
    ln1_bias,
    w_in,
    b_in,
    w_out,
    b_out,
    ln2_gain,
    ln2_bias,
    cotangent,
):
    seq_count, local_len, model_width = tokens.shape
    (
        proj_qkv,
        bias_qv,
        proj_attn,
        bias_attn,
        gain_first,
        shift_first,
        proj_in,
        bias_in,
        proj_out,
        bias_out,
        gain_second,
        shift_second,
    ) = (
        lax.all_gather(w_qkv, "fsdp", axis=1, tiled=True),
        lax.all_gather(b_qv, "fsdp", axis=2, tiled=True),
        lax.all_gather(w_o, "fsdp", axis=1, tiled=True),
        lax.all_gather(b_o, "fsdp", axis=0, tiled=True),
        lax.all_gather(ln1_gain, "fsdp", axis=0, tiled=True),
        lax.all_gather(ln1_bias, "fsdp", axis=0, tiled=True),
        lax.all_gather(w_in, "fsdp", axis=0, tiled=True),
        lax.all_gather(b_in, "fsdp", axis=1, tiled=True),
        lax.all_gather(w_out, "fsdp", axis=1, tiled=True),
        lax.all_gather(b_out, "fsdp", axis=0, tiled=True),
        lax.all_gather(ln2_gain, "fsdp", axis=0, tiled=True),
        lax.all_gather(ln2_bias, "fsdp", axis=0, tiled=True),
    )
    local_width = proj_qkv.shape[2]
    head_size = bias_qv.shape[2]
    local_heads = local_width // head_size
    row_count = seq_count * local_len
    inputs = tokens.reshape(row_count, model_width)
    gain_one = gain_first.astype(jnp.float32)
    shift_one = shift_first.astype(jnp.float32)
    gain_two = gain_second.astype(jnp.float32)
    shift_two = shift_second.astype(jnp.float32)

    def finish_sum(partial_rows):
        return lax.psum(partial_rows.astype(jnp.bfloat16), "tp").astype(jnp.float32)

    projected = jnp.einsum("rd,kdc->krc", inputs, proj_qkv, preferred_element_type=jnp.float32)
    query_rows = (projected[0] + bias_qv[0].reshape(-1).astype(jnp.float32)).astype(jnp.bfloat16)
    key_blocks = projected[1].astype(jnp.bfloat16).reshape(seq_count, local_len, local_width)
    value_blocks = (
        (projected[2] + bias_qv[1].reshape(-1).astype(jnp.float32))
        .astype(jnp.bfloat16)
        .reshape(seq_count, local_len, local_width)
    )
    key_all, value_all = (
        lax.all_gather(key_blocks, "ctx", axis=1, tiled=True),
        lax.all_gather(value_blocks, "ctx", axis=1, tiled=True),
    )
    block_start = lax.axis_index("ctx") * local_len
    query_segments = lax.dynamic_slice_in_dim(segments, block_start, local_len, 1)
    same_doc = query_segments[:, :, None] == segments[:, None, :]
    query_heads = to_heads(query_rows.reshape(seq_count, local_len, local_width), head_size)
    key_heads = to_heads(key_all, head_size)
    value_heads = to_heads(value_all, head_size)

    def attend_head(operands):
        query_head, key_head, value_head = operands
        scores = masked_scores(query_head, key_head, same_doc)
        row_max = jnp.max(scores, -1, keepdims=True)
        exp_scores = jnp.exp(scores - row_max)
        denominator = jnp.sum(exp_scores, -1, keepdims=True)
        probs_low = (exp_scores / denominator).astype(jnp.bfloat16)
        mixed_rows = jnp.einsum(
            "sqk,skd->sqd", probs_low, value_head, preferred_element_type=jnp.float32
        )
        return (mixed_rows.astype(jnp.bfloat16), row_max, denominator)

    attended_heads, row_maxes, denominators = lax.map(
        attend_head, (query_heads, key_heads, value_heads)
    )
    attended_rows = from_heads(attended_heads).reshape(row_count, local_width)
    attn_part = jnp.dot(attended_rows, proj_attn, preferred_element_type=jnp.float32)
    attn_rows = finish_sum(attn_part) + bias_attn.astype(jnp.float32)
    first_in = inputs.astype(jnp.float32) + attn_rows
    normed = layer_norm(first_in, gain_one, shift_one)
    normed_low = normed.astype(jnp.bfloat16)
    pre_act = jnp.dot(normed_low, proj_in, preferred_element_type=jnp.float32) + bias_in.reshape(
        -1
    ).astype(jnp.float32)
    act_low = gelu_exact(pre_act).astype(jnp.bfloat16)
    mlp_part = jnp.dot(act_low, proj_out, preferred_element_type=jnp.float32)
    mlp_rows = finish_sum(mlp_part) + bias_out.astype(jnp.float32)
    second_in = normed + mlp_rows
    final_rows = layer_norm(second_in, gain_two, shift_two)
    output = final_rows.astype(jnp.bfloat16).reshape(seq_count, local_len, model_width)
    grad_final = cotangent.reshape(row_count, model_width).astype(jnp.float32)
    unused_second, pull_second = jax.vjp(layer_norm, second_in, gain_two, shift_two)
    grad_second, grad_gain_second, grad_shift_second = pull_second(grad_final)
    grad_mlp = grad_second.astype(jnp.bfloat16)
    grad_bias_out = jnp.sum(grad_mlp, 0, dtype=jnp.float32)
    grad_proj_out = jnp.einsum("rf,rd->fd", act_low, grad_mlp, preferred_element_type=jnp.float32)
    grad_act = jnp.einsum("rd,fd->rf", grad_mlp, proj_out, preferred_element_type=jnp.float32)
    unused_gelu, pull_gelu = jax.vjp(gelu_exact, pre_act)
    grad_pre = pull_gelu(grad_act)[0].astype(jnp.bfloat16)
    grad_bias_in = jnp.sum(grad_pre, 0, dtype=jnp.float32).reshape(bias_in.shape)
    grad_proj_in = jnp.einsum("rd,rf->df", normed_low, grad_pre, preferred_element_type=jnp.float32)
    back_part = jnp.einsum("rf,df->rd", grad_pre, proj_in, preferred_element_type=jnp.float32)
    grad_normed = grad_second + finish_sum(back_part)
    unused_first, pull_first = jax.vjp(layer_norm, first_in, gain_one, shift_one)
    grad_first, grad_gain_first, grad_shift_first = pull_first(grad_normed)
    grad_attn = grad_first.astype(jnp.bfloat16)
    grad_bias_attn = jnp.sum(grad_attn, 0, dtype=jnp.float32)
    grad_proj_attn = jnp.einsum(
        "rc,rd->cd", attended_rows, grad_attn, preferred_element_type=jnp.float32
    )
    grad_attended = jnp.einsum(
        "rd,cd->rc", grad_attn, proj_attn, preferred_element_type=jnp.float32
    ).astype(jnp.bfloat16)
    grad_att_heads = to_heads(grad_attended.reshape(seq_count, local_len, local_width), head_size)
    key_again, value_again = (
        lax.all_gather(key_blocks, "ctx", axis=1, tiled=True),
        lax.all_gather(value_blocks, "ctx", axis=1, tiled=True),
    )
    key_back = to_heads(key_again, head_size)
    value_back = to_heads(value_again, head_size)

    def head_grads(operands):
        query_head, key_head, value_head, grad_head, row_max, denominator = operands
        scores = masked_scores(query_head, key_head, same_doc)
        attn_probs = jnp.exp(scores - row_max) / denominator
        probs_low = attn_probs.astype(jnp.bfloat16)
        grad_probs = jnp.einsum(
            "sqd,skd->sqk", grad_head, value_head, preferred_element_type=jnp.float32
        )
        row_delta = jnp.sum(attn_probs * grad_probs, -1, keepdims=True)
        grad_scores = (attn_probs * (grad_probs - row_delta)).astype(jnp.bfloat16)
        grad_query = (
            jnp.einsum("sqk,skd->sqd", grad_scores, key_head, preferred_element_type=jnp.float32)
            * SCALE_QK
        )
        grad_key = (
            jnp.einsum("sqk,sqd->skd", grad_scores, query_head, preferred_element_type=jnp.float32)
            * SCALE_QK
        )
        grad_value = jnp.einsum(
            "sqk,sqd->skd", probs_low, grad_head, preferred_element_type=jnp.float32
        )
        return (grad_query.astype(jnp.bfloat16), grad_key, grad_value)

    grad_query_heads, grad_key_heads, grad_value_heads = lax.map(
        head_grads, (query_heads, key_back, value_back, grad_att_heads, row_maxes, denominators)
    )
    grad_key_full = from_heads(grad_key_heads)
    grad_value_full = from_heads(grad_value_heads)
    grad_key_part, grad_value_part = (
        lax.psum_scatter(
            grad_key_full.astype(jnp.bfloat16), "ctx", scatter_dimension=1, tiled=True
        ).astype(jnp.float32),
        lax.psum_scatter(
            grad_value_full.astype(jnp.bfloat16), "ctx", scatter_dimension=1, tiled=True
        ).astype(jnp.float32),
    )
    grad_query_rows = from_heads(grad_query_heads).reshape(row_count, local_width)
    grad_key_rows = grad_key_part.astype(jnp.bfloat16).reshape(row_count, local_width)
    grad_value_rows = grad_value_part.astype(jnp.bfloat16).reshape(row_count, local_width)
    grad_stack = jnp.stack([grad_query_rows, grad_key_rows, grad_value_rows])
    grad_proj_qkv = jnp.einsum(
        "rd,krc->kdc", inputs, grad_stack, preferred_element_type=jnp.float32
    )
    grad_bias_qv = jnp.stack(
        [
            jnp.sum(grad_query_rows, 0, dtype=jnp.float32),
            jnp.sum(grad_value_rows, 0, dtype=jnp.float32),
        ]
    ).reshape(2, local_heads, head_size)
    input_part = jnp.einsum("krc,kdc->rd", grad_stack, proj_qkv, preferred_element_type=jnp.float32)
    grad_inputs = grad_first + finish_sum(input_part)
    grad_tokens = grad_inputs.astype(jnp.bfloat16).reshape(seq_count, local_len, model_width)
    (
        share_qkv,
        share_bqv,
        share_attn,
        share_battn,
        share_gone,
        share_sone,
        share_in,
        share_bin,
        share_out,
        share_bout,
        share_gtwo,
        share_stwo,
    ) = (
        lax.psum_scatter(grad_proj_qkv, ("fsdp", "ctx"), scatter_dimension=1, tiled=True),
        lax.psum_scatter(grad_bias_qv, ("fsdp", "ctx"), scatter_dimension=2, tiled=True),
        lax.psum_scatter(grad_proj_attn, ("fsdp", "ctx"), scatter_dimension=1, tiled=True),
        lax.psum_scatter(grad_bias_attn, ("fsdp", "ctx"), scatter_dimension=0, tiled=True),
        lax.psum_scatter(grad_gain_first, ("fsdp", "ctx"), scatter_dimension=0, tiled=True),
        lax.psum_scatter(grad_shift_first, ("fsdp", "ctx"), scatter_dimension=0, tiled=True),
        lax.psum_scatter(grad_proj_in, ("fsdp", "ctx"), scatter_dimension=0, tiled=True),
        lax.psum_scatter(grad_bias_in, ("fsdp", "ctx"), scatter_dimension=1, tiled=True),
        lax.psum_scatter(grad_proj_out, ("fsdp", "ctx"), scatter_dimension=1, tiled=True),
        lax.psum_scatter(grad_bias_out, ("fsdp", "ctx"), scatter_dimension=0, tiled=True),
        lax.psum_scatter(grad_gain_second, ("fsdp", "ctx"), scatter_dimension=0, tiled=True),
        lax.psum_scatter(grad_shift_second, ("fsdp", "ctx"), scatter_dimension=0, tiled=True),
    )
    reduced = (
        lax.all_gather(share_qkv.astype(jnp.bfloat16), "ctx", axis=1, tiled=True).astype(
            share_qkv.dtype
        ),
        lax.all_gather(share_bqv.astype(jnp.bfloat16), "ctx", axis=2, tiled=True).astype(
            share_bqv.dtype
        ),
        lax.all_gather(share_attn.astype(jnp.bfloat16), "ctx", axis=1, tiled=True).astype(
            share_attn.dtype
        ),
        lax.all_gather(share_battn.astype(jnp.bfloat16), "ctx", axis=0, tiled=True).astype(
            share_battn.dtype
        ),
        lax.all_gather(share_gone.astype(jnp.bfloat16), "ctx", axis=0, tiled=True).astype(
            share_gone.dtype
        ),
        lax.all_gather(share_sone.astype(jnp.bfloat16), "ctx", axis=0, tiled=True).astype(
            share_sone.dtype
        ),
        lax.all_gather(share_in.astype(jnp.bfloat16), "ctx", axis=0, tiled=True).astype(
            share_in.dtype
        ),
        lax.all_gather(share_bin.astype(jnp.bfloat16), "ctx", axis=1, tiled=True).astype(
            share_bin.dtype
        ),
        lax.all_gather(share_out.astype(jnp.bfloat16), "ctx", axis=1, tiled=True).astype(
            share_out.dtype
        ),
        lax.all_gather(share_bout.astype(jnp.bfloat16), "ctx", axis=0, tiled=True).astype(
            share_bout.dtype
        ),
        lax.all_gather(share_gtwo.astype(jnp.bfloat16), "ctx", axis=0, tiled=True).astype(
            share_gtwo.dtype
        ),
        lax.all_gather(share_stwo.astype(jnp.bfloat16), "ctx", axis=0, tiled=True).astype(
            share_stwo.dtype
        ),
    )
    return (
        output,
        grad_tokens,
        reduced[0],
        reduced[1],
        reduced[2],
        reduced[3],
        reduced[4],
        reduced[5],
        reduced[6],
        reduced[7],
        reduced[8],
        reduced[9],
        reduced[10],
        reduced[11],
    )


def solution(mesh):
    in_specs = (
        P("fsdp", "ctx", None),
        P("fsdp", None),
        P(None, "fsdp", "tp"),
        P(None, "tp", "fsdp"),
        P("tp", "fsdp"),
        P("fsdp"),
        P("fsdp"),
        P("fsdp"),
        P("fsdp", "tp"),
        P("tp", "fsdp"),
        P("tp", "fsdp"),
        P("fsdp"),
        P("fsdp"),
        P("fsdp"),
        P("fsdp", "ctx", None),
    )
    out_specs = (
        P("fsdp", "ctx", None),
        P("fsdp", "ctx", None),
        P(None, "fsdp", "tp"),
        P(None, "tp", "fsdp"),
        P("tp", "fsdp"),
        P("fsdp"),
        P("fsdp"),
        P("fsdp"),
        P("fsdp", "tp"),
        P("tp", "fsdp"),
        P("tp", "fsdp"),
        P("fsdp"),
        P("fsdp"),
        P("fsdp"),
    )
    return jax.shard_map(local, mesh=mesh, in_specs=in_specs, out_specs=out_specs, check_vma=False)
```

profile of v0, /device:TPU:0, one launch (start us, length us, event | category | flops | bytes accessed | tf_op | source)
XLA Modules:
  0.0 1384.4 jit_solution(14793995309170661180)
XLA Ops:
  10.4 5.4 all_gather.81
  16.0 24.1 %all-gather.21.cloned.1.call-done = bf16[3,1024,256]{1,2,0:T(8,128)(2,1)} async-done(((bf16[3,512,256]{1,2,0:T(8,128)(2,1)}), bf16[3,1024,256]{1,2,0:T(8,128)(2,1)}) %all-gather.21.cloned.1.call-update) | async-done | bytes 1572880 | tf_op jit(solution)/shard_map/all_gather | solution.py:73
  40.0 5.7 convolution_bitcast_fusion
  58.1 8.9 all_gather.84
  71.3 17.5 %all-gather.25.cloned.1.call-done = bf16[4,2048,256]{1,2,0:T(8,128)(2,1)} async-done(((bf16[4,512,256]{1,2,0:T(8,128)(2,1)}), bf16[4,2048,256]{1,2,0:T(8,128)(2,1)}) %all-gather.25.cloned.1.call-update) | async-done | bytes 4194320 | tf_op jit(solution)/shard_map/all_gather | solution.py:109
  93.5 31.9 %all-gather.23.cloned.1.call-done = bf16[4,2048,256]{1,2,0:T(8,128)(2,1)} async-done(((bf16[4,512,256]{1,2,0:T(8,128)(2,1)}), bf16[4,2048,256]{1,2,0:T(8,128)(2,1)}) %all-gather.23.cloned.1.call-update) | async-done | bytes 4194320 | tf_op jit(solution)/shard_map/all_gather | solution.py:108
  130.3 62.6 %while.30 = (s32[]{:T(128)}, bf16[4,4,512,64]{2,3,1,0:T(8,128)(2,1)S(1)}, f32[4,4,512,1]{2,1,3,0:T(4,128)}, f32[4,4,512,1]{2,1,3,0:T(4,128)}, bf16[4,4,512,64]{2...) while((s32[]{:T(128)}, ...), condition=%wide.region_3.4_spmd.clone, body=%wide.region_0.3_spmd.clone.sunk | while | flops 1136783360 | bytes 53152356 | solution.py:130
  139.8 6.2 fusion.121
  155.4 6.2 fusion.121
  171.1 6.2 fusion.121
  186.7 6.2 fusion.121
  217.5 136.0 %all-reduce.14.cloned.1.call-done = bf16[2048,1024]{1,0:T(8,128)(2,1)} async-done(((bf16[2048,1024]{1,0:T(8,128)(2,1)}), bf16[2048,1024]{1,0:T(8,128)(2,1)}) %all-reduce.14.cloned.1.call-update) | async-done | bytes 4194320 | tf_op jit(solution)/shard_map/psum | solution.py:97
  364.1 22.9 %all-gather.27.cloned.1.call-done = bf16[1024,1024]{1,0:T(8,128)(2,1)} async-done(((bf16[512,1024]{1,0:T(8,128)(2,1)}), bf16[1024,1024]{1,0:T(8,128)(2,1)}) %all-gather.27.cloned.1.call-update) | async-done | bytes 2097168 | tf_op jit(solution)/shard_map/all_gather | solution.py:79
  387.0 11.0 multiply_convert_fusion.1
  398.0 23.6 %all-gather.29.cloned.1.call-done = bf16[1024,1024]{1,0:T(8,128)(2,1)} async-done(((bf16[1024,512]{1,0:T(8,128)(2,1)}), bf16[1024,1024]{1,0:T(8,128)(2,1)}) %all-gather.29.cloned.1.call-update) | async-done | bytes 2097168 | tf_op jit(solution)/shard_map/all_gather | solution.py:81
  421.5 9.4 convolution_convert_fusion.2
  444.7 141.4 %all-reduce.16.cloned.1.call-done = bf16[2048,1024]{1,0:T(8,128)(2,1)} async-done(((bf16[2048,1024]{1,0:T(8,128)(2,1)}), bf16[2048,1024]{1,0:T(8,128)(2,1)}) %all-reduce.16.cloned.1.call-update) | async-done | bytes 4194320 | tf_op jit(solution)/shard_map/psum | solution.py:97
  586.1 5.8 fusion.76
  598.0 5.4 fusion.75
  606.5 12.3 convert_reduce_fusion.2
  620.8 6.3 convolution_convert_fusion.1
  627.3 10.0 fusion.81
  637.4 11.4 fusion.69
  648.9 132.4 %all-reduce.18.cloned.1.call-done = bf16[2048,1024]{1,0:T(8,128)(2,1)} async-done(((bf16[2048,1024]{1,0:T(8,128)(2,1)}), bf16[2048,1024]{1,0:T(8,128)(2,1)}) %all-reduce.18.cloned.1.call-update) | async-done | bytes 4194320 | tf_op jit(solution)/shard_map/psum | solution.py:97
  781.2 9.4 multiply_reduce_fusion.1
  790.7 8.8 fusion.74
  810.9 182.2 %while.31 = (s32[]{:T(128)}, bf16[4,4,512,64]{2,3,1,0:T(8,128)(2,1)}, bf16[4,4,2048,64]{2,3,0,1:T(8,128)(2,1)}, bf16[4,4,2048,64]{2,3,0,1:T(8,128)(2,1)}, bf16[4...) while((s32[]{:T(128)}, ...), condition=%wide.region_17.18_spmd.clone, body=%wide.region_15.17_spmd.clone.sunk | while | flops 2731276288 | bytes 202223824 | solution.py:202
  812.2 9.4 fusion.128
  822.3 9.8 multiply_reduce_fusion.6
  832.0 7.1 multiply_convert_fusion.3
  846.9 7.8 fusion.129
  858.3 9.4 fusion.128
  868.4 9.8 multiply_reduce_fusion.6
  878.2 7.3 multiply_convert_fusion.3
  893.3 7.0 fusion.129
  903.9 9.4 fusion.128
  914.0 9.7 multiply_reduce_fusion.6
  923.7 7.0 multiply_convert_fusion.3
  938.4 7.0 fusion.129
  949.0 9.4 fusion.128
  959.1 9.7 multiply_reduce_fusion.6
  968.9 7.0 multiply_convert_fusion.3
  983.6 7.0 fusion.129
  1007.2 29.6 %reduce-scatter.9.cloned.1.call-done = bf16[4,512,256]{1,2,0:T(8,128)(2,1)} async-done(((bf16[4,2048,256]{1,2,0:T(8,128)(2,1)}), bf16[4,512,256]{1,2,0:T(8,128)(2,1)}) %reduce-scatter.9.cloned.1.call-update) | async-done | bytes 1048592 | tf_op jit(solution)/shard_map/reduce_scatter | solution.py:208
  1038.3 45.3 %reduce-scatter.11.cloned.1.call-done = bf16[4,512,256]{1,2,0:T(8,128)(2,1)} async-done(((bf16[4,2048,256]{1,2,0:T(8,128)(2,1)}), bf16[4,512,256]{1,2,0:T(8,128)(2,1)}) %reduce-scatter.11.cloned.1.call-update) | async-done | bytes 1048592 | tf_op jit(solution)/shard_map/reduce_scatter | solution.py:211
  1085.1 6.3 bitcast_convert_fusion
  1091.5 7.5 convolution_bitcast_fusion.1
  1105.4 18.0 %reduce-scatter.15.cloned.1.call-done = f32[256,128]{1,0:T(8,128)} async-done(((f32[256,1024]{1,0:T(8,128)}), f32[256,128]{1,0:T(8,128)}) %reduce-scatter.15.cloned.1.call-update) | async-done | bytes 131088 | tf_op jit(solution)/shard_map/reduce_scatter | solution.py:247
  1124.3 5.8 all_gather.96
  1130.9 10.7 all-gather.33.cloned.1.call-done
  1144.5 15.9 %all-gather.31.cloned.1.call-done = bf16[512,1024]{1,0:T(8,128)(2,1)} async-done(((bf16[128,1024]{1,0:T(8,128)(2,1)}), bf16[512,1024]{1,0:T(8,128)(2,1)}) %all-gather.31.cloned.1.call-update) | async-done | bytes 1048592 | tf_op jit(solution)/shard_map/all_gather | solution.py:277
  1163.5 25.0 %all-reduce.8 = (bf16[2,4,64]{2,1,0:T(4,128)(2,1)S(1)}, bf16[16,64]{1,0:T(8,128)(2,1)S(1)}, bf16[1024]{0:T(1024)(128)(2,1)S(1)}, bf16[1024]{0:T(1024)(128)(2,1)S...) all-reduce(f32[2,4,64]{2,1,0:T(4,128)S(1)} %pad_maximum_fusion.3, ...), channel_id=5, replica_groups=mesh['fsdp'=2,'ctx'=4,'tp'=4] {'fsdp','ctx'}, use_global_device_ids=true, to_apply=%region_24.25.clone | all-reduce | flops 7680 | bytes 46080
  1188.6 5.2 all_gather.95
  1194.7 5.2 all_gather.101
  1200.6 5.0 all-gather.7
  1206.3 5.0 all-gather.8
  1212.0 5.0 all-gather.9
  1217.7 5.0 all-gather.10
  1223.4 5.0 all-gather.11
  1229.1 5.0 all-gather.12
  1234.7 83.4 %all-reduce.20.cloned.1.call-done = bf16[2048,1024]{1,0:T(8,128)(2,1)} async-done(((bf16[2048,1024]{1,0:T(8,128)(2,1)}), bf16[2048,1024]{1,0:T(8,128)(2,1)}) %all-reduce.20.cloned.1.call-update) | async-done | bytes 4194320 | tf_op jit(solution)/shard_map/psum | solution.py:97
  1318.2 7.1 add_convert_fusion
  1325.3 41.2 %reduce-scatter.13.cloned.1.call-done = f32[3,128,256]{1,2,0:T(8,128)} async-done(((f32[3,1024,256]{1,2,0:T(8,128)}), f32[3,128,256]{1,2,0:T(8,128)}) %reduce-scatter.13.cloned.1.call-update) | async-done | bytes 393232 | tf_op jit(solution)/shard_map/reduce_scatter | solution.py:245
  1367.5 8.6 all_gather.94
  (265 shorter events, 224.9 us)
Async XLA Ops:
  7.2 32.9 %all-gather.21.cloned.1.call-start = ((), (), s32[]{:S(2)}) async-start(), calls=%async_computation.6 | async-start | bytes 2359296 | tf_op jit(solution)/shard_map/all_gather | solution.py:73
  9.5 79.2 %all-gather.25.cloned.1.call-start = ((), (), s32[]{:S(2)}) async-start(), calls=%async_computation.8 | async-start | bytes 5242880 | tf_op jit(solution)/shard_map/all_gather | solution.py:109
  45.8 4.0 copy-start.9
  49.8 8.3 copy-start.16
  49.8 8.3 copy-start.20
  54.2 71.2 %all-gather.23.cloned.1.call-start = ((), (), s32[]{:S(2)}) async-start(), calls=%async_computation.7 | async-start | bytes 5242880 | tf_op jit(solution)/shard_map/all_gather | solution.py:108
  57.9 295.6 %all-reduce.14.cloned.1.call-start = ((), (), s32[]{:S(2)}) async-start(), calls=%async_computation.9 | async-start | bytes 8388608 | tf_op jit(solution)/shard_map/psum | solution.py:97
  130.3 64.7 %copy-start.15 = (bf16[256,1024]{1,0:T(8,128)(2,1)S(1)}, bf16[256,1024]{1,0:T(8,128)(2,1)}, u32[]{:S(2)}) copy-start(bf16[256,1024]{1,0:T(8,128)(2,1)} %all_gather.84) | copy-start | bytes 1572868
  192.9 5.5 copy-start.18
  193.7 5.9 copy-start.30
  193.7 10.2 copy-start.31
  193.8 14.6 %copy-start.32 = (bf16[512]{0:T(512)(128)(2,1)S(1)}, bf16[512]{0:T(512)(128)(2,1)}, u32[]{:S(2)}) copy-start(bf16[512]{0:T(512)(128)(2,1)} %param.26) | copy-start | bytes 3076
  193.8 19.0 %copy-start.28 = (bf16[16,32]{1,0:T(8,128)(2,1)S(1)}, bf16[16,32]{1,0:T(8,128)(2,1)}, u32[]{:S(2)}) copy-start(bf16[16,32]{1,0:T(8,128)(2,1)} %param.28) | copy-start | bytes 3076
  198.4 188.6 %all-gather.27.cloned.1.call-start = ((), (), s32[]{:S(2)}) async-start(), calls=%async_computation.10 | async-start | bytes 3145728 | tf_op jit(solution)/shard_map/all_gather | solution.py:79
  199.0 222.6 %all-gather.29.cloned.1.call-start = ((), (), s32[]{:S(2)}) async-start(), calls=%async_computation.11 | async-start | bytes 3145728 | tf_op jit(solution)/shard_map/all_gather | solution.py:81
  199.5 386.6 %all-reduce.16.cloned.1.call-start = ((), (), s32[]{:S(2)}) async-start(), calls=%async_computation.12 | async-start | bytes 8388608 | tf_op jit(solution)/shard_map/psum | solution.py:97
  353.5 5.0 copy-start.5
  353.5 5.9 copy-start.6
  421.5 9.5 copy-start.33
  421.5 13.9 %copy-start.34 = (bf16[512]{0:T(512)(128)(2,1)S(1)}, bf16[512]{0:T(512)(128)(2,1)}, u32[]{:S(2)}) copy-start(bf16[512]{0:T(512)(128)(2,1)} %param.31) | copy-start | bytes 3076
  421.5 18.3 %copy-start.35 = (bf16[512]{0:T(512)(128)(2,1)S(1)}, bf16[512]{0:T(512)(128)(2,1)}, u32[]{:S(2)}) copy-start(bf16[512]{0:T(512)(128)(2,1)} %param.32) | copy-start | bytes 3076
  431.0 350.2 %all-reduce.18.cloned.1.call-start = ((), (), s32[]{:S(2)}) async-start(), calls=%async_computation.13 | async-start | bytes 8388608 | tf_op jit(solution)/shard_map/psum | solution.py:97
  591.9 2.2 copy-start.3
  603.4 15.5 %copy-start.1 = (f32[2048,1024]{1,0:T(8,128)}, f32[2048,1024]{1,0:T(8,128)S(1)}, u32[]{:S(2)}) copy-start(f32[2048,1024]{1,0:T(8,128)S(1)} %get-tuple-element.391) | copy-start | bytes 25165828
  603.4 3.1 copy-start.37
  604.8 14.0 %copy-start.11 = (bf16[2048,1024]{1,0:T(8,128)(2,1)}, bf16[2048,1024]{1,0:T(8,128)(2,1)S(1)}, u32[]{:S(2)}) copy-start(bf16[2048,1024]{1,0:T(8,128)(2,1)S(1)} %get-tuple-element.383) | copy-start | bytes 12582916
  606.5 14.3 %copy-start.36 = (bf16[1024,1024]{1,0:T(8,128)(2,1)S(1)}, bf16[1024,1024]{1,0:T(8,128)(2,1)}, u32[]{:S(2)}) copy-start(bf16[1024,1024]{1,0:T(8,128)(2,1)} %all-gather.27.cloned.1.call-done) | copy-start | bytes 6291460
  618.8 2.0 copy-start.39
  627.1 371.7 %reduce-scatter.19.cloned.1.call-start = ((), (), s32[]{:S(2)}) async-start(), calls=%async_computation.21 | async-start | bytes 4718592 | tf_op jit(solution)/shard_map/reduce_scatter | solution.py:253
  637.3 363.4 %reduce-scatter.17.cloned.1.call-start = ((), (), s32[]{:S(2)}) async-start(), calls=%async_computation.19 | async-start | bytes 4718592 | tf_op jit(solution)/shard_map/reduce_scatter | solution.py:251
  648.8 388.0 %reduce-scatter.9.cloned.1.call-start = ((), (), s32[]{:S(2)}) async-start(), calls=%async_computation.14 | async-start | bytes 5242880 | tf_op jit(solution)/shard_map/reduce_scatter | solution.py:208
  781.2 9.5 copy-start.4
  799.5 3.2 copy-start.2
  799.6 4.7 copy-start.21
  804.2 2.1 copy-start.10
  804.2 6.7 copy-start.17
  804.2 6.7 copy-start.19
  832.0 10.3 copy-start.12
  839.1 3.2 copy-start
  844.9 1.9 copy-start.13
  878.2 10.6 copy-start.12
  885.5 3.2 copy-start
  891.4 1.9 copy-start.13
  923.7 10.2 copy-start.12
  930.7 3.2 copy-start
  936.5 1.9 copy-start.13
  968.9 10.2 copy-start.12
  975.8 3.2 copy-start
  981.6 1.9 copy-start.13
  993.1 90.5 %reduce-scatter.11.cloned.1.call-start = ((), (), s32[]{:S(2)}) async-start(), calls=%async_computation.15 | async-start | bytes 5242880 | tf_op jit(solution)/shard_map/reduce_scatter | solution.py:211
  993.7 129.6 %reduce-scatter.15.cloned.1.call-start = ((), (), s32[]{:S(2)}) async-start(), calls=%async_computation.18 | async-start | bytes 1179648 | tf_op jit(solution)/shard_map/reduce_scatter | solution.py:247
  998.8 142.8 %all-gather.33.cloned.1.call-start = ((), (), s32[]{:S(2)}) async-start(), calls=%async_computation.22 | async-start | bytes 1310720 | tf_op jit(solution)/shard_map/all_gather | solution.py:283
  1000.6 159.7 %all-gather.31.cloned.1.call-start = ((), (), s32[]{:S(2)}) async-start(), calls=%async_computation.20 | async-start | bytes 1310720 | tf_op jit(solution)/shard_map/all_gather | solution.py:277
  1002.6 315.5 %all-reduce.20.cloned.1.call-start = ((), (), s32[]{:S(2)}) async-start(), calls=%async_computation.16 | async-start | bytes 8388608 | tf_op jit(solution)/shard_map/psum | solution.py:97
  1091.5 7.6 copy-start.38
  1091.5 12.4 copy-start.29
  1091.5 274.9 %reduce-scatter.13.cloned.1.call-start = ((), (), s32[]{:S(2)}) async-start(), calls=%async_computation.17 | async-start | bytes 3538944 | tf_op jit(solution)/shard_map/reduce_scatter | solution.py:245
  1099.0 64.1 %copy-start.14 = (bf16[4,512,256]{1,2,0:T(8,128)(2,1)S(1)}, bf16[4,512,256]{1,2,0:T(8,128)(2,1)}, u32[]{:S(2)}) copy-start(bf16[4,512,256]{1,2,0:T(8,128)(2,1)} %reduce-scatter.11.cloned.1.call-done) | copy-start | bytes 3145732
  1099.0 64.4 %copy-start.23 = (f32[1024]{0:T(1024)S(1)}, f32[1024]{0:T(1024)}, u32[]{:S(2)}) copy-start(f32[1024]{0:T(1024)} %get-tuple-element.382) | copy-start | bytes 12292
  1099.0 64.4 %copy-start.24 = (f32[1024]{0:T(1024)S(1)}, f32[1024]{0:T(1024)}, u32[]{:S(2)}) copy-start(f32[1024]{0:T(1024)} %get-tuple-element.384) | copy-start | bytes 12292
  1099.0 64.4 %copy-start.25 = (f32[1024]{0:T(1024)S(1)}, f32[1024]{0:T(1024)}, u32[]{:S(2)}) copy-start(f32[1024]{0:T(1024)} %get-tuple-element.329) | copy-start | bytes 12292
  1099.0 64.4 %copy-start.26 = (f32[1024]{0:T(1024)S(1)}, f32[1024]{0:T(1024)}, u32[]{:S(2)}) copy-start(f32[1024]{0:T(1024)} %get-tuple-element.327) | copy-start | bytes 12292
  1099.0 64.4 %copy-start.27 = (f32[1024]{0:T(1024)S(1)}, f32[1024]{0:T(1024)}, u32[]{:S(2)}) copy-start(f32[1024]{0:T(1024)} %get-tuple-element.331) | copy-start | bytes 12292
  1099.1 219.1 %copy-start.22 = (f32[2048]{0:T(1024)S(1)}, f32[2048]{0:T(1024)}, u32[]{:S(2)}) copy-start(f32[2048]{0:T(1024)} %copy-done.21) | copy-start | bytes 24580
  (2 other events, 2.2 us)
Sparse Core Ops, SparseCore 0:
  10.1 29.8 all-gather.20
  54.3 34.4 all-gather.24
  90.9 34.4 all-gather.22
  198.5 154.9 all-reduce.13
  354.9 32.0 all-gather.26
  388.4 33.0 all-gather.28
  431.1 154.9 all-reduce.15
  627.2 153.9 all-reduce.17
  784.6 50.0 reduce-scatter.18
  837.9 51.1 reduce-scatter.16
  993.3 43.4 reduce-scatter.8
  1039.2 44.3 reduce-scatter.10
  1087.4 35.9 reduce-scatter.14
  1124.8 16.8 all-gather.32
  1143.6 16.6 all-gather.30
  1163.1 155.0 all-reduce.19
  1321.4 45.0 reduce-scatter.12
where the time goes:
time: 1390 us; the launch traced here: 1380 us
  waiting for transfers between devices  776 us (56%)
  matrix products  257 us (18%)
  blocking collectives  126 us (9%)
  other arithmetic  123 us (9%)
  local copies, waits for them, and re-layouts  85 us (6%)
  between operations  16.3 us (1%)
    psum x4, waiting for transfers between devices, finish_sum(): return lax.psum(partial_rows.astype(jnp.bfloat16), 'tp').astype(jnp.float32)  493 us
    dot_general x8, matrix products, masked_scores(): jnp.einsum('sqd,skd->sqk', query_head, key_head, preferred_element_type=j...  56.8 us
    reduce_scatter x1, waiting for transfers between devices, local(): lax.psum_scatter(grad_value_full.astype(jnp.bfloat16), 'ctx', scatter_dim...  45.3 us
    reduce_scatter x1, waiting for transfers between devices, local(): lax.psum_scatter(grad_proj_qkv, ('fsdp', 'ctx'), scatter_dimension=1, til...  41.2 us
    dot_general x4, matrix products, head_grads(): jnp.einsum('sqd,skd->sqk', grad_head, value_head, preferred_element_type=...  37.4 us
    all_gather x1, waiting for transfers between devices, local(): lax.all_gather(key_blocks, 'ctx', axis=1, tiled=True)  31.9 us
    unnamed x97, local copies, waits for them, and re-layouts  30.6 us
    reduce_scatter x1, waiting for transfers between devices, local(): lax.psum_scatter(grad_key_full.astype(jnp.bfloat16), 'ctx', scatter_dimen...  29.6 us
  transfers between devices with their start and end apart: 17, of which 15 were waited for; matrix products, arithmetic and copies ran while one was open for 21% of the time, Pallas kernels for 0%

commit v1 on v0

--- a/solution.py
+++ b/solution.py
@@ -94,7 +94,9 @@
     shift_two = shift_second.astype(jnp.float32)
 
     def finish_sum(partial_rows):
-        return lax.psum(partial_rows.astype(jnp.bfloat16), "tp").astype(jnp.float32)
+        return jnp.sum(lax.all_gather(partial_rows.astype(jnp.bfloat16), "tp"), axis=0).astype(
+            jnp.float32
+        )
 
     projected = jnp.einsum("rd,kdc->krc", inputs, proj_qkv, preferred_element_type=jnp.float32)
     query_rows = (projected[0] + bias_qv[0].reshape(-1).astype(jnp.float32)).astype(jnp.bfloat16)

time: 1390 us -> 1970 us (1.42)
  waiting for transfers between devices: 776 us -> 1310 us
  other arithmetic: 123 us -> 180 us
  local copies, waits for them, and re-layouts: 85 us -> 60.3 us
    all_gather x0 -> x4, waiting for transfers between devices: none -> 1090 us  [finish_sum(): lax.all_gather(partial_rows.astype(jnp.bfloat16), 'tp')]
    psum x4 -> x0, waiting for transfers between devices: 493 us -> none  [finish_sum(): return lax.psum(partial_rows.astype(jnp.bfloat16), 'tp').astype(jnp.float32)]
    reduce_sum x1 -> x4, other arithmetic: 1.46 us -> 49.4 us  [finish_sum(): jnp.sum(lax.all_gather(partial_rows.astype(jnp.bfloat16), 'tp'), axis=0)]
    all_gather x1, waiting for transfers between devices: 31.9 us -> 8.94 us  [local(): lax.all_gather(key_blocks, 'ctx', axis=1, tiled=True)]
    while x24, local copies, waits for them, and re-layouts: 20.6 us -> 0.44 us
  transfers between devices with their start and end apart: 17 -> 17, of which waited for: 15 -> 13; matrix products, arithmetic and copies ran while one was open for 21% -> 18% of each run, Pallas kernels for 0% -> 0%
where the time goes in v1:
time: 1970 us; the launch traced here: 1960 us
  waiting for transfers between devices  1310 us (66%)
  matrix products  270 us (14%)
  other arithmetic  180 us (9%)
  blocking collectives  123 us (6%)
  local copies, waits for them, and re-layouts  60.3 us (3%)
    all_gather x4, waiting for transfers between devices, finish_sum(): lax.all_gather(partial_rows.astype(jnp.bfloat16), 'tp')  1090 us
    dot_general x8, matrix products, masked_scores(): jnp.einsum('sqd,skd->sqk', query_head, key_head, preferred_element_type=j...  57.4 us
    reduce_sum x4, other arithmetic, finish_sum(): jnp.sum(lax.all_gather(partial_rows.astype(jnp.bfloat16), 'tp'), axis=0)  49.4 us
    reduce_scatter x1, waiting for transfers between devices, local(): lax.psum_scatter(grad_value_full.astype(jnp.bfloat16), 'ctx', scatter_dim...  45.3 us
  transfers between devices with their start and end apart: 17, of which 13 were waited for; matrix products, arithmetic and copies ran while one was open for 18% of the time, Pallas kernels for 0%

profile of v1, /device:TPU:0, one launch (start us, length us, event | category | flops | bytes accessed | tf_op | source)
XLA Modules:
  0.0 1961.4 jit_solution(12715843704382153071)
XLA Ops:
  9.6 30.5 %all-gather.29.cloned.1.call-done = bf16[3,1024,256]{1,2,0:T(8,128)(2,1)} async-done(((bf16[3,512,256]{1,2,0:T(8,128)(2,1)}), bf16[3,1024,256]{1,2,0:T(8,128)(2,1)}) %all-gather.29.cloned.1.call-update) | async-done | bytes 1572880 | tf_op jit(solution)/shard_map/all_gather | solution.py:73
  40.1 5.7 convolution_bitcast_fusion
  55.4 5.2 fusion.94
  65.1 7.7 all_gather.108
  76.2 8.9 all-gather.31.cloned.1.call-done
  90.0 31.8 %all-gather.33.cloned.1.call-done = bf16[4,2048,256]{1,2,0:T(8,128)(2,1)} async-done(((bf16[4,512,256]{1,2,0:T(8,128)(2,1)}), bf16[4,2048,256]{1,2,0:T(8,128)(2,1)}) %all-gather.33.cloned.1.call-update) | async-done | bytes 4194320 | tf_op jit(solution)/shard_map/all_gather | solution.py:111
  126.6 63.2 %while.30 = (s32[]{:T(128)}, bf16[4,4,512,64]{2,3,1,0:T(8,128)(2,1)S(1)}, f32[4,4,512,1]{2,1,3,0:T(4,128)}, f32[4,4,512,1]{2,1,3,0:T(4,128)}, bf16[4,4,512,64]{2...) while((s32[]{:T(128)}, ...), condition=%wide.region_3.4_spmd.clone, body=%wide.region_0.3_spmd.clone.sunk | while | flops 1136783360 | bytes 53151856 | solution.py:132
  135.6 6.2 fusion.134
  151.4 6.2 fusion.134
  167.3 6.2 fusion.134
  183.1 6.2 fusion.134
  215.5 267.8 %all-gather.43.cloned.1.call-done = bf16[8192,1024]{1,0:T(8,128)(2,1)} async-done(((bf16[2048,1024]{1,0:T(8,128)(2,1)}), bf16[8192,1024]{1,0:T(8,128)(2,1)}) %all-gather.43.cloned.1.call-update) | async-done | bytes 16777232 | tf_op jit(solution)/shard_map/all_gather | solution.py:97
  483.3 12.6 reduce_sum.232
  516.0 10.9 multiply_convert_fusion.1
  526.9 23.6 %all-gather.37.cloned.1.call-done = bf16[1024,1024]{1,0:T(8,128)(2,1)} async-done(((bf16[1024,512]{1,0:T(8,128)(2,1)}), bf16[1024,1024]{1,0:T(8,128)(2,1)}) %all-gather.37.cloned.1.call-update) | async-done | bytes 2097168 | tf_op jit(solution)/shard_map/all_gather | solution.py:81
  550.5 9.4 convolution_convert_fusion.2
  569.0 277.9 %all-gather.45.cloned.1.call-done = bf16[8192,1024]{1,0:T(8,128)(2,1)} async-done(((bf16[2048,1024]{1,0:T(8,128)(2,1)}), bf16[8192,1024]{1,0:T(8,128)(2,1)}) %all-gather.45.cloned.1.call-update) | async-done | bytes 16777232 | tf_op jit(solution)/shard_map/all_gather | solution.py:97
  846.8 12.1 reduce_sum.235
  858.9 6.1 fusion.92
  877.2 12.5 convert_reduce_fusion.1
  891.7 6.4 convolution_convert_fusion.1
  898.5 11.5 fusion.63
  914.5 11.7 fusion.86
  926.4 256.7 %all-gather.47.cloned.1.call-done = bf16[8192,1024]{1,0:T(8,128)(2,1)} async-done(((bf16[2048,1024]{1,0:T(8,128)(2,1)}), bf16[8192,1024]{1,0:T(8,128)(2,1)}) %all-gather.47.cloned.1.call-update) | async-done | bytes 16777232 | tf_op jit(solution)/shard_map/all_gather | solution.py:97
  1183.2 12.3 reduce_sum.280
  1195.5 15.2 multiply_reduce_fusion.1
  1210.7 7.1 fusion.91
  1218.4 7.5 fusion.57
  1228.5 171.5 %while.31 = (s32[]{:T(128)}, bf16[4,4,512,64]{2,3,1,0:T(8,128)(2,1)}, bf16[4,4,2048,64]{2,3,0,1:T(8,128)(2,1)}, bf16[4,4,2048,64]{2,3,0,1:T(8,128)(2,1)}, bf16[4...) while((s32[]{:T(128)}, ...), condition=%wide.region_17.18_spmd.clone, body=%wide.region_15.17_spmd.clone.sunk | while | flops 2731276288 | bytes 177057008 | solution.py:204
  1229.6 9.3 fusion.141
  1239.0 9.8 multiply_reduce_fusion.8
  1248.7 10.0 multiply_convert_fusion.3
  1261.2 7.2 fusion.142
  1272.8 9.5 fusion.141
  1282.4 9.7 multiply_reduce_fusion.8
  1292.1 9.4 multiply_convert_fusion.3
  1304.1 7.1 fusion.142
  1315.7 9.3 fusion.141
  1325.0 9.8 multiply_reduce_fusion.8
  1334.8 9.4 multiply_convert_fusion.3
  1346.7 7.1 fusion.142
  1358.3 9.3 fusion.141
  1367.7 9.7 multiply_reduce_fusion.8
  1377.4 9.4 multiply_convert_fusion.3
  1389.4 7.1 fusion.142
  1408.2 35.9 %reduce-scatter.9.cloned.1.call-done = bf16[4,512,256]{1,2,0:T(8,128)(2,1)} async-done(((bf16[4,2048,256]{1,2,0:T(8,128)(2,1)}), bf16[4,512,256]{1,2,0:T(8,128)(2,1)}) %reduce-scatter.9.cloned.1.call-update) | async-done | bytes 1048592 | tf_op jit(solution)/shard_map/reduce_scatter | solution.py:210
  1445.6 45.3 %reduce-scatter.11.cloned.1.call-done = bf16[4,512,256]{1,2,0:T(8,128)(2,1)} async-done(((bf16[4,2048,256]{1,2,0:T(8,128)(2,1)}), bf16[4,512,256]{1,2,0:T(8,128)(2,1)}) %reduce-scatter.11.cloned.1.call-update) | async-done | bytes 1048592 | tf_op jit(solution)/shard_map/reduce_scatter | solution.py:213
  1493.2 7.6 bitcast_convert_fusion
  1500.9 7.7 convolution_bitcast_fusion.1
  1513.4 15.2 all-gather.39.cloned.1.call-done
  1531.5 286.0 %all-gather.49.cloned.1.call-done = bf16[8192,1024]{1,0:T(8,128)(2,1)} async-done(((bf16[2048,1024]{1,0:T(8,128)(2,1)}), bf16[8192,1024]{1,0:T(8,128)(2,1)}) %all-gather.49.cloned.1.call-update) | async-done | bytes 16777232 | tf_op jit(solution)/shard_map/all_gather | solution.py:97
  1817.5 12.4 reduce_sum.284
  1829.8 7.4 convert_reduce_fusion.2
  1840.1 24.8 %reduce-scatter.13.cloned.1.call-done = f32[3,128,256]{1,2,0:T(8,128)} async-done(((f32[3,1024,256]{1,2,0:T(8,128)}), f32[3,128,256]{1,2,0:T(8,128)}) %reduce-scatter.13.cloned.1.call-update) | async-done | bytes 393232 | tf_op jit(solution)/shard_map/reduce_scatter | solution.py:247
  1866.0 8.9 all_gather.126
  1876.3 24.2 %all-reduce.8 = (bf16[2,4,64]{2,1,0:T(4,128)(2,1)S(1)}, bf16[16,64]{1,0:T(8,128)(2,1)S(1)}, bf16[1024]{0:T(1024)(128)(2,1)S(1)}, bf16[1024]{0:T(1024)(128)(2,1)S...) all-reduce(f32[2,4,64]{2,1,0:T(4,128)S(1)} %pad_maximum_fusion.3, ...), channel_id=9, replica_groups=mesh['fsdp'=2,'ctx'=4,'tp'=4] {'fsdp','ctx'}, use_global_device_ids=true, to_apply=%region_24.25.clone | all-reduce | flops 7680 | bytes 46080
  1900.7 5.0 all-gather.16
  1906.4 5.0 all-gather.15
  1912.1 5.0 all-gather.14
  1917.8 5.0 all-gather.13
  1923.5 5.0 all-gather.12
  1935.0 5.2 all_gather.133
  1940.9 5.2 all_gather.127
  1947.7 5.9 all_gather.128
  (288 shorter events, 208.7 us)
Async XLA Ops:
  7.2 32.9 %all-gather.29.cloned.1.call-start = ((), (), s32[]{:S(2)}) async-start(), calls=%async_computation.6 | async-start | bytes 2359296 | tf_op jit(solution)/shard_map/all_gather | solution.py:73
  9.5 75.6 %all-gather.31.cloned.1.call-start = ((), (), s32[]{:S(2)}) async-start(), calls=%async_computation.7 | async-start | bytes 5242880 | tf_op jit(solution)/shard_map/all_gather | solution.py:110
  40.0 10.6 copy-start.32
  45.8 2.6 copy-start.15
  50.6 71.2 %all-gather.33.cloned.1.call-start = ((), (), s32[]{:S(2)}) async-start(), calls=%async_computation.8 | async-start | bytes 5242880 | tf_op jit(solution)/shard_map/all_gather | solution.py:111
  55.4 9.7 copy-start.19
  55.4 9.7 copy-start.23
  64.9 418.4 %all-gather.43.cloned.1.call-start = ((), (), s32[]{:S(2)}) async-start(), calls=%async_computation.19 | async-start | bytes 20971520 | tf_op jit(solution)/shard_map/all_gather | solution.py:97
  189.9 6.5 copy-start.14
  189.9 6.5 copy-start.21
  190.7 6.9 copy-start.33
  190.7 11.3 copy-start.34
  190.7 15.7 copy-start.35
  190.7 20.1 %copy-start.30 = (bf16[16,32]{1,0:T(8,128)(2,1)S(1)}, bf16[16,32]{1,0:T(8,128)(2,1)}, u32[]{:S(2)}) copy-start(bf16[16,32]{1,0:T(8,128)(2,1)} %param.28) | copy-start | bytes 3076
  196.4 319.6 %all-gather.35.cloned.1.call-start = ((), (), s32[]{:S(2)}) async-start(), calls=%async_computation.9 | async-start | bytes 3145728 | tf_op jit(solution)/shard_map/all_gather | solution.py:79
  197.0 353.5 %all-gather.37.cloned.1.call-start = ((), (), s32[]{:S(2)}) async-start(), calls=%async_computation.10 | async-start | bytes 3145728 | tf_op jit(solution)/shard_map/all_gather | solution.py:81
  197.6 649.3 %all-gather.45.cloned.1.call-start = ((), (), s32[]{:S(2)}) async-start(), calls=%async_computation.20 | async-start | bytes 20971520 | tf_op jit(solution)/shard_map/all_gather | solution.py:97
  500.8 4.3 copy-start.1
  500.8 5.4 copy-start.5
  500.8 6.5 copy-start.8
  550.5 9.5 copy-start.36
  550.5 13.8 copy-start.37
  559.9 623.2 %all-gather.47.cloned.1.call-start = ((), (), s32[]{:S(2)}) async-start(), calls=%async_computation.21 | async-start | bytes 20971520 | tf_op jit(solution)/shard_map/all_gather | solution.py:97
  858.9 6.2 copy-start.3
  865.1 5.2 copy-start.2
  865.1 5.2 slice-start
  867.5 4.0 copy-start.4
  867.6 5.2 slice-start.1
  872.7 4.4 copy-start.40
  877.2 12.5 copy-start.6
  877.2 14.5 copy-start.39
  898.1 12.1 copy-start.38
  898.1 502.6 %reduce-scatter.19.cloned.1.call-start = ((), (), s32[]{:S(2)}) async-start(), calls=%async_computation.17 | async-start | bytes 4718592 | tf_op jit(solution)/shard_map/reduce_scatter | solution.py:255
  910.0 492.5 %reduce-scatter.17.cloned.1.call-start = ((), (), s32[]{:S(2)}) async-start(), calls=%async_computation.15 | async-start | bytes 4718592 | tf_op jit(solution)/shard_map/reduce_scatter | solution.py:253
  926.2 517.9 %reduce-scatter.9.cloned.1.call-start = ((), (), s32[]{:S(2)}) async-start(), calls=%async_computation.11 | async-start | bytes 5242880 | tf_op jit(solution)/shard_map/reduce_scatter | solution.py:210
  1210.7 7.7 copy-start.7
  1210.7 7.7 copy-start.17
  1218.4 10.1 copy-start.20
  1218.4 10.1 copy-start.22
  1261.2 7.2 copy-start
  1261.2 10.7 copy-start.13
  1304.1 7.1 copy-start
  1304.1 10.7 copy-start.13
  1346.7 7.1 copy-start
  1346.7 10.6 copy-start.13
  1389.4 7.1 copy-start
  1389.4 10.6 copy-start.13
  1400.0 4.4 copy-start.9
  1400.0 90.9 %reduce-scatter.11.cloned.1.call-start = ((), (), s32[]{:S(2)}) async-start(), calls=%async_computation.12 | async-start | bytes 5242880 | tf_op jit(solution)/shard_map/reduce_scatter | solution.py:213
  1400.6 110.0 %all-gather.41.cloned.1.call-start = ((), (), s32[]{:S(2)}) async-start(), calls=%async_computation.18 | async-start | bytes 1310720 | tf_op jit(solution)/shard_map/all_gather | solution.py:285
  1402.5 126.2 %all-gather.39.cloned.1.call-start = ((), (), s32[]{:S(2)}) async-start(), calls=%async_computation.16 | async-start | bytes 1310720 | tf_op jit(solution)/shard_map/all_gather | solution.py:279
  1404.4 413.1 %all-gather.49.cloned.1.call-start = ((), (), s32[]{:S(2)}) async-start(), calls=%async_computation.22 | async-start | bytes 20971520 | tf_op jit(solution)/shard_map/all_gather | solution.py:97
  1493.2 7.7 copy-start.18
  1500.8 7.8 copy-start.41
  1500.8 9.7 copy-start.31
  1500.8 364.1 %reduce-scatter.13.cloned.1.call-start = ((), (), s32[]{:S(2)}) async-start(), calls=%async_computation.13 | async-start | bytes 3538944 | tf_op jit(solution)/shard_map/reduce_scatter | solution.py:247
  1508.6 438.2 %reduce-scatter.15.cloned.1.call-start = ((), (), s32[]{:S(2)}) async-start(), calls=%async_computation.14 | async-start | bytes 1179648 | tf_op jit(solution)/shard_map/reduce_scatter | solution.py:249
  1817.5 12.4 copy-start.24
  1829.8 7.4 copy-start.11
  1837.2 39.1 %copy-start.25 = (f32[1024]{0:T(1024)S(1)}, f32[1024]{0:T(1024)}, u32[]{:S(2)}) copy-start(f32[1024]{0:T(1024)} %get-tuple-element.329) | copy-start | bytes 12292
  1837.2 39.1 %copy-start.26 = (f32[1024]{0:T(1024)S(1)}, f32[1024]{0:T(1024)}, u32[]{:S(2)}) copy-start(f32[1024]{0:T(1024)} %get-tuple-element.330) | copy-start | bytes 12292
  1837.2 39.1 %copy-start.27 = (f32[1024]{0:T(1024)S(1)}, f32[1024]{0:T(1024)}, u32[]{:S(2)}) copy-start(f32[1024]{0:T(1024)} %get-tuple-element.334) | copy-start | bytes 12292
  1837.2 39.1 %copy-start.28 = (f32[1024]{0:T(1024)S(1)}, f32[1024]{0:T(1024)}, u32[]{:S(2)}) copy-start(f32[1024]{0:T(1024)} %get-tuple-element.402) | copy-start | bytes 12292
  1837.2 39.0 %copy-start.29 = (f32[1024]{0:T(1024)S(1)}, f32[1024]{0:T(1024)}, u32[]{:S(2)}) copy-start(f32[1024]{0:T(1024)} %get-tuple-element.404) | copy-start | bytes 12292
  (7 other events, 9.4 us)
Sparse Core Ops, SparseCore 0:
  10.1 29.8 all-gather.28
  50.7 34.4 all-gather.30
  87.3 34.4 all-gather.32
  196.5 286.7 all-gather.42
  484.7 31.2 all-gather.34
  517.4 33.0 all-gather.36
  560.1 286.7 all-gather.44
  898.2 284.9 all-gather.46
  1186.5 49.2 reduce-scatter.18
  1239.0 51.1 reduce-scatter.16
  1400.1 43.9 reduce-scatter.8
  1446.5 44.3 reduce-scatter.10
  1493.1 16.8 all-gather.40
  1511.9 16.7 all-gather.38
  1530.7 286.7 all-gather.48
  1820.7 44.2 reduce-scatter.12
  1868.0 36.0 reduce-scatter.14
